TPU v7x, 32 devices: a whole 2x2x4 slice. The times are simulated.
32 devices in a mesh: grp: 2 (over y), wide: 16 (over z, x, core).
Axes of the slice: x: 2, y: 2, z: 4, core: 2. Of those that a mesh axis runs over, the one named last changes fastest.
Arguments:
- activations: bfloat16 [2, 1024, 4096], P('grp', 'wide'), parts along dimension 0, may hold values from -6 to 6
- output_grads: bfloat16 [2, 1024, 4096], P('grp', None, 'wide'), parts along dimension 0, may hold values from -0.1875 to 0.1875
- token_ids: int32 [2, 1024], P('grp'), parts along dimension 0, may hold values from 0 to 128255, as said below
- row_signs: int32 [4096], replicated, may hold values from -1 to 1, as said below
- column_signs: int32 [4096], replicated, may hold values from -1 to 1, as said below
- kept_blocks: int32 [8192], P('wide'), may hold values from 0 to 131071, as said below
- queries: bfloat16 [256, 1048576], P(None, 'wide'), may hold values from -0.0078125 to 0.0078125
Outputs:
- sketches: bfloat16 [2, 1048576], P('grp', 'wide'), parts along dimension 0
- scores: float32 [256, 2], P('wide', 'grp'), parts along dimension 1
There are 2 independent parts, one for each index of `grp`. A program takes and returns all parts, laid end to end along the dimension named above; an argument that names none is the same for every part. Nothing has to cross between parts.
Inputs may be any that keep to these rules, and one draw needn't show every extreme that they name: `token_ids`: id 0 marks padding. Each sequence ends with one run of one or more padding ids, and 512 or more of its ids are 1 or more. `row_signs`: every entry is +1 or -1. `column_signs`: every entry is +1 or -1. `kept_blocks`: A block number b names column b // 32 and rows (b % 32) * 128 up to (b % 32 + 1) * 128 - 1 of a sequence's projected matrix. For every d, entries d * 512 up to (d + 1) * 512 - 1 are distinct and name columns d * 256 up to (d + 1) * 256 - 1.
All inputs are finite; a program needn't handle non-finite values.
Results may differ from a plain program's by a relative error of at most 0.006.
Values may be sent and summed in bfloat16 or wider, within the bound.
A program may use at most 256 MiB of HBM per device.

v0:
```python
import jax
import jax.numpy as jnp
from jax import lax
from jax.sharding import PartitionSpec as P

ROWBLK = 128


def sign_table(bit_count):
    length = 2**bit_count
    indices = jnp.arange(length, dtype=jnp.int32)
    common = jnp.bitwise_and(indices[:, None], indices[None, :])
    parity = jnp.zeros((length, length), jnp.int32)
    for position in range(bit_count):
        parity = parity + jnp.bitwise_and(jnp.right_shift(common, position), 1)
    signs = 1 - 2 * jnp.bitwise_and(parity, 1)
    return (signs.astype(jnp.float32) * length ** (-0.5)).astype(jnp.bfloat16)


def hadamard_table(order_size):
    total_bits = order_size.bit_length() - 1
    low_bits = total_bits // 2
    high_table = sign_table(total_bits - low_bits)
    low_table = sign_table(low_bits)
    high_table, low_table = lax.optimization_barrier((high_table, low_table))
    return (high_table[:, None, :, None] * low_table[None, :, None, :]).reshape(
        order_size, order_size
    )


def per_device(activations, output_grads, token_ids, row_signs, column_signs, kept_blocks, queries):
    model_width = column_signs.shape[0]
    hadamard = hadamard_table(model_width)
    row_blocks = model_width // ROWBLK
    column_sign = column_signs.astype(jnp.bfloat16)
    row_sign = row_signs.astype(jnp.bfloat16)
    weight = (token_ids != 0).astype(jnp.bfloat16)
    columns_dev = output_grads.shape[2]
    device = lax.axis_index("wide")
    local_blocks = kept_blocks - device * (columns_dev * row_blocks)
    turned = jnp.einsum(
        "stj,jk->stk",
        activations * column_sign[None, None, :],
        hadamard,
        preferred_element_type=jnp.float32,
    ).astype(jnp.bfloat16)
    columns = lax.all_to_all(turned, "wide", split_axis=2, concat_axis=1, tiled=True)
    weighted = columns * weight[:, :, None]
    half_turned = jnp.einsum(
        "stc,sti->sci",
        weighted,
        lax.all_gather(output_grads, "wide", axis=2, tiled=True),
        preferred_element_type=jnp.float32,
    ).astype(jnp.bfloat16)
    signed = half_turned * row_sign[None, None, :]
    projected = jnp.einsum("scj,ji->sci", signed, hadamard, preferred_element_type=jnp.float32)
    items = projected.shape[0]
    block_rows = projected.reshape(items, projected.shape[1] * row_blocks, ROWBLK)
    picked = jnp.take(block_rows, local_blocks, axis=1)
    sketches = picked.reshape(items, picked.shape[1] * ROWBLK).astype(jnp.bfloat16)
    scores = lax.psum_scatter(
        jnp.einsum("qc,sc->qs", queries, sketches, preferred_element_type=jnp.float32),
        "wide",
        scatter_dimension=0,
        tiled=True,
    )
    return (sketches, scores)


def solution(mesh):
    placed = (
        P("grp", "wide", None),
        P("grp", None, "wide"),
        P("grp", None),
        P(),
        P(),
        P("wide"),
        P(None, "wide"),
    )
    return jax.shard_map(
        per_device,
        mesh=mesh,
        in_specs=placed,
        out_specs=(P("grp", "wide"), P("wide", "grp")),
        check_vma=False,
    )
```

profile of v0, /device:TPU:0, one launch (start us, length us, event | category | flops | bytes accessed | tf_op | source)
XLA Modules:
  0.0 292.9 jit_solution(1452810544550997973)
XLA Ops:
  7.2 0.0 all-gather.2.cloned.1.call-start
  7.2 0.7 all-gather.2.cloned.1.call-update
  7.9 21.2 %broadcast_multiply_fusion = bf16[64,64,64,64]{3,2,1,0:T(8,128)(2,1)} fusion(bf16[64,64]{1,0:T(8,128)(2,1)S(1)} %multiply_convert_fusion), kind=kLoop, calls=%fused_computation.1 | loop fusion | flops 16777216 | bytes 33562624 | tf_op jit(solution)/shard_map/mul | solution.py:26
  29.1 0.0 copy-start.1
  29.1 0.0 copy-start
  29.1 87.2 %mul.83 = bf16[4096,4096]{1,0:T(8,128)(2,1)} reshape(bf16[64,64,64,64]{3,2,1,0:T(8,128)(2,1)} %broadcast_multiply_fusion) | data formatting | bytes 67108864 | tf_op jit(solution)/shard_map/mul | solution.py:26
  116.3 0.0 copy-done.1
  116.3 0.0 copy-done
  116.3 13.6 %fusion.8 = bf16[1,64,4096]{2,1,0:T(8,128)(2,1)S(1)} fusion(bf16[4096,4096]{1,0:T(8,128)(2,1)} %mul.83, bf16[1,64,4096]{2,1,0:T(8,128)(2,1)S(1)} %copy-done, bf16[4096]{0:T(1024)(128)(2,1)S(1)} %convert_element_type.43), kind=kOutput, calls=%fused_computation.7 | convolution fusion | flops 2148007936 | bytes 34611200 | tf_op jit(solution)/shard_map/stj,jk->stk/dot_general | solution.py:41
  130.0 0.0 copy-start.3
  130.0 0.0 copy-start.2
  130.0 0.0 copy-start.4
  130.0 2.8 copy.12
  132.8 0.5 broadcast.80
  133.3 22.4 %reduce.2 = bf16[4096,64]{1,0:T(8,128)(2,1)S(1)} reduce(bf16[4096,1,64]{2,1,0:T(2,128)(2,1)S(1)} %bitcast.56, bf16[]{:T(256)} %broadcast.80), dimensions={1}, to_apply=%bitcast.47.reduce_sub_computation | reduce | bytes 1048578
  155.7 1.5 reshape.131
  157.2 7.4 %all-to-all-start = ((bf16[16,2,8192]{2,1,0:T(2,128)(2,1)}), bf16[16,2,8192]{2,1,0:T(2,128)(2,1)S(1)}, u32[]{:S(2)}, u32[]{:S(2)}) async-start(bf16[16,2,8192]{2,1,0:T(2,128)(2,1)} %reshape.131), calls=%async_computation | async-start | bytes 1048576 | tf_op jit(solution)/shard_map/all_to_all | solution.py:47
  164.7 0.2 reduce-scatter.4.cloned.1.call-start
  164.9 0.0 copy-done.3
  164.9 0.1 reshape.111
  165.0 0.1 copy.14
  165.1 0.0 copy-done.2
  165.1 0.0 copy-done.4
  165.2 0.1 broadcast_bitcast_fusion
  165.3 13.6 %all-to-all-done = bf16[16,2,8192]{2,1,0:T(2,128)(2,1)S(1)} async-done(((bf16[16,2,8192]{2,1,0:T(2,128)(2,1)}), bf16[16,2,8192]{2,1,0:T(2,128)(2,1)S(1)}, u32[]{:S(2)}, u32[]{:S(2)}) %all-to-all-start) | async-done | bytes 524320 | tf_op jit(solution)/shard_map/all_to_all | solution.py:47
  178.9 1.2 reshape.132
  180.2 2.3 copy.13
  182.5 0.1 copy.19
  182.6 0.2 fusion.13
  182.8 0.2 copy.15
  182.9 0.0 all-gather.2.cloned.1.call-done
  183.0 22.9 %fusion.10 = f32[256,4096]{1,0:T(8,128)} fusion(bf16[4096,4096]{1,0:T(8,128)(2,1)} %mul.83, bf16[1024,256]{1,0:T(8,128)(2,1)S(1)} %bitcast.60, bf16[1,1024,4096]{2,1,0:T(8,128)(2,1)} %all-gather.2.cloned.1.call-done, bf16[4096]{0:T(1024)(128)(2,1)S(1)} %convert_element_type.49), kind=kOutput, calls=%fused_computation.8 | convolution fusion | flops 10739515392 | bytes 46669824 | tf_op jit(solution)/shard_map/scj,ji->sci/dot_general | solution.py:56
  205.9 4.9 %reshape.112 = f32[8192,128]{1,0:T(8,128)} reshape(f32[256,4096]{1,0:T(8,128)} %fusion.10) | data formatting | bytes 8388608 | tf_op jit(solution)/shard_map/reshape | solution.py:58
  210.8 3.2 %gather_fusion = f32[512,128]{1,0:T(8,128)S(1)} fusion(f32[8192,128]{1,0:T(8,128)} %reshape.112, s32[1024]{0:T(1024)S(1)} %pad_clamp_fusion), kind=kCustom, calls=%fused_computation | custom fusion | bytes 526336 | tf_op jit(solution)/shard_map/jit(_take)/gather | solution.py:59
  214.1 0.1 fusion.17
  214.2 0.1 reshape.126
  214.3 15.1 %convolution_bitcast_fusion = f32[256,1]{1,0:T(8,128)} fusion(bf16[65536,1]{0,1:T(2,128)(2,1)S(1)} %reshape.126, bf16[256,65536]{1,0:T(8,128)(2,1)} %param.13), kind=kOutput, calls=%fused_computation.9 | convolution fusion | flops 33554432 | bytes 33686528 | tf_op jit(solution)/shard_map/qc,sc->qs/dot_general | solution.py:62
  229.4 0.0 reduce-scatter.4.cloned.1.call-update
  229.5 1.1 fusion.16
  230.6 54.2 %reduce-scatter.4.cloned.1.call-done = f32[16,1]{1,0:T(8,128)} async-done(((f32[256,1]{1,0:T(8,128)}), f32[16,1]{1,0:T(8,128)}) %reduce-scatter.4.cloned.1.call-update) | async-done | bytes 80
  284.8 1.3 copy.17
  (6 shorter events, 0.1 us)
Async XLA Ops:
  7.2 175.8 %all-gather.2.cloned.1.call-start = ((), (), s32[]{:S(2)}) async-start(), calls=%async_computation.2 | async-start | bytes 8912896 | tf_op jit(solution)/shard_map/all_gather | solution.py:52
  29.1 87.2 %copy-start.1 = (s32[4096]{0:T(1024)S(1)}, s32[4096]{0:T(1024)}, u32[]{:S(2)}) copy-start(s32[4096]{0:T(1024)} %param.11) | copy-start | bytes 49156
  29.1 87.2 %copy-start = (bf16[1,64,4096]{2,1,0:T(8,128)(2,1)S(1)}, bf16[1,64,4096]{2,1,0:T(8,128)(2,1)}, u32[]{:S(2)}) copy-start(bf16[1,64,4096]{2,1,0:T(8,128)(2,1)} %param.7) | copy-start | bytes 1572868
  130.0 34.9 %copy-start.3 = (s32[1,1024]{1,0:T(1,128)S(1)}, s32[1,1024]{1,0:T(1,128)}, u32[]{:S(2)}) copy-start(s32[1,1024]{1,0:T(1,128)} %param.9) | copy-start | bytes 12292
  130.0 35.2 %copy-start.2 = (s32[4096]{0:T(1024)S(1)}, s32[4096]{0:T(1024)}, u32[]{:S(2)}) copy-start(s32[4096]{0:T(1024)} %param.10) | copy-start | bytes 49156
  130.0 35.2 %copy-start.4 = (s32[512]{0:T(512)S(1)}, s32[512]{0:T(512)}, u32[]{:S(2)}) copy-start(s32[512]{0:T(512)} %param.12) | copy-start | bytes 6148
  157.2 21.7 %all-to-all-start = ((bf16[16,2,8192]{2,1,0:T(2,128)(2,1)}), bf16[16,2,8192]{2,1,0:T(2,128)(2,1)S(1)}, u32[]{:S(2)}, u32[]{:S(2)}) async-start(bf16[16,2,8192]{2,1,0:T(2,128)(2,1)} %reshape.131), calls=%async_computation | async-start | bytes 1048576 | tf_op jit(solution)/shard_map/all_to_all | solution.py:47
  164.7 120.1 %reduce-scatter.4.cloned.1.call-start = ((), (), s32[]{:S(2)}) async-start(), calls=%async_computation.3 | async-start | bytes 139264
Sparse Core Ops, SparseCore 0:
  10.1 80.4 all-gather.1
  229.6 55.1 reduce-scatter.3
where the time goes:
time: 296 us; the launch traced here: 293 us
  local copies, waits for them, and re-layouts  106 us (36%)
  waiting for transfers between devices  68.6 us (23%)
  matrix products  51.7 us (17%)
  other arithmetic  45.1 us (15%)
  between operations  14.2 us (5%)
  starting transfers between devices  7.7 us (3%)
    mul x1, local copies, waits for them, and re-layouts, hadamard_table(): high_table[:, None, :, None] * low_table[None, :, None, :]  87.2 us
    unnamed x3, waiting for transfers between devices  54.9 us
    dot_general x1, matrix products, per_device(): jnp.einsum('scj,ji->sci', signed, hadamard, preferred_element_type=jnp.fl...  22.9 us
    unnamed x1, other arithmetic  22.4 us
    mul x1, other arithmetic, hadamard_table(): high_table[:, None, :, None] * low_table[None, :, None, :]  21.2 us
    dot_general x1, matrix products, per_device(): jnp.einsum('qc,sc->qs', queries, sketches, preferred_element_type=jnp.flo...  15.1 us
    dot_general x1, matrix products, per_device(): jnp.einsum('stj,jk->stk', activations * column_sign[None, None, :], hadam...  13.6 us
    all_to_all x1, waiting for transfers between devices, per_device(): lax.all_to_all(turned, 'wide', split_axis=2, concat_axis=1, tiled=True)  13.6 us
  transfers between devices with their start and end apart: 3, of which 2 were waited for; matrix products, arithmetic and copies ran while one was open for 53% of the time, Pallas kernels for 0%

commit v1 on v0

--- a/solution.py
+++ b/solution.py
@@ -44,7 +44,10 @@
         hadamard,
         preferred_element_type=jnp.float32,
     ).astype(jnp.bfloat16)
-    columns = lax.all_to_all(turned, "wide", split_axis=2, concat_axis=1, tiled=True)
+    columns = jnp.concatenate(
+        lax.all_to_all(jnp.stack(jnp.split(turned, lax.axis_size("wide"), axis=2)), "wide", 0, 0),
+        axis=1,
+    )
     weighted = columns * weight[:, :, None]
     half_turned = jnp.einsum(
         "stc,sti->sci",

time: 296 us -> 274 us (0.926)
  other arithmetic: 45.1 us -> 22.7 us
    unnamed x1 -> x0, other arithmetic: 22.4 us -> none
    unnamed x16 -> x27, local copies, waits for them, and re-layouts: 4.79 us -> 10.7 us
  transfers between devices with their start and end apart: 3 -> 3, of which waited for: 2 -> 2; matrix products, arithmetic and copies ran while one was open for 53% -> 49% of each run, Pallas kernels for 0% -> 0%
where the time goes in v1:
time: 274 us; the launch traced here: 272 us
  local copies, waits for them, and re-layouts  107 us (39%)
  waiting for transfers between devices  68.7 us (25%)
  matrix products  51.7 us (19%)
  other arithmetic  22.7 us (8%)
  between operations  14.2 us (5%)
  starting transfers between devices  7.7 us (3%)
    mul x1, local copies, waits for them, and re-layouts, hadamard_table(): high_table[:, None, :, None] * low_table[None, :, None, :]  87.2 us
    unnamed x3, waiting for transfers between devices  55 us
    dot_general x1, matrix products, per_device(): jnp.einsum('scj,ji->sci', signed, hadamard, preferred_element_type=jnp.fl...  22.9 us
    mul x1, other arithmetic, hadamard_table(): high_table[:, None, :, None] * low_table[None, :, None, :]  21.2 us
    dot_general x1, matrix products, per_device(): jnp.einsum('qc,sc->qs', queries, sketches, preferred_element_type=jnp.flo...  15.1 us
    all_to_all x1, waiting for transfers between devices, per_device(): lax.all_to_all(jnp.stack(jnp.split(turned, lax.axis_size('wide'), axis=2)...  13.7 us
    dot_general x1, matrix products, per_device(): jnp.einsum('stj,jk->stk', activations * column_sign[None, None, :], hadam...  13.6 us
    unnamed x27, local copies, waits for them, and re-layouts  10.7 us
  transfers between devices with their start and end apart: 3, of which 2 were waited for; matrix products, arithmetic and copies ran while one was open for 49% of the time, Pallas kernels for 0%

profile of v1, /device:TPU:0, one launch (start us, length us, event | category | flops | bytes accessed | tf_op | source)
XLA Modules:
  0.0 271.7 jit_solution(11914816879175366050)
XLA Ops:
  7.2 0.0 all-gather.2.cloned.1.call-start
  7.2 0.7 all-gather.2.cloned.1.call-update
  7.9 21.2 %broadcast_multiply_fusion = bf16[64,64,64,64]{3,2,1,0:T(8,128)(2,1)} fusion(bf16[64,64]{1,0:T(8,128)(2,1)S(1)} %multiply_convert_fusion), kind=kLoop, calls=%fused_computation.1 | loop fusion | flops 16777216 | bytes 33562624 | tf_op jit(solution)/shard_map/mul | solution.py:26
  29.1 0.0 copy-start.1
  29.1 0.0 copy-start
  29.1 87.2 %mul.83 = bf16[4096,4096]{1,0:T(8,128)(2,1)} reshape(bf16[64,64,64,64]{3,2,1,0:T(8,128)(2,1)} %broadcast_multiply_fusion) | data formatting | bytes 67108864 | tf_op jit(solution)/shard_map/mul | solution.py:26
  116.3 0.0 copy-done.1
  116.3 0.0 copy-start.3
  116.3 0.0 copy-start.2
  116.3 0.0 copy-start.4
  116.3 0.0 copy-done
  116.3 13.6 %fusion.8 = bf16[1,64,4096]{2,1,0:T(8,128)(2,1)S(1)} fusion(bf16[4096,4096]{1,0:T(8,128)(2,1)} %mul.83, bf16[1,64,4096]{2,1,0:T(8,128)(2,1)S(1)} %copy-done, bf16[4096]{0:T(1024)(128)(2,1)S(1)} %convert_element_type.43), kind=kOutput, calls=%fused_computation.7 | convolution fusion | flops 2148007936 | bytes 34611200 | tf_op jit(solution)/shard_map/stj,jk->stk/dot_general | solution.py:41
  130.0 0.6 fusion.33
  130.6 0.6 fusion.32
  131.2 0.6 fusion.31
  131.8 0.6 fusion.30
  132.4 0.6 fusion.29
  133.1 0.6 fusion.28
  133.7 0.6 fusion.27
  134.3 0.6 fusion.26
  134.9 0.6 fusion.25
  135.5 0.6 fusion.24
  136.1 0.6 fusion.23
  136.7 0.6 fusion.22
  137.4 0.6 fusion.21
  138.0 0.6 fusion.20
  138.6 0.6 fusion.19
  139.2 0.6 fusion.18
  139.8 7.4 %all-to-all-start = ((bf16[16,1,64,256]{3,2,1,0:T(8,128)(2,1)}), bf16[16,1,64,256]{3,2,1,0:T(8,128)(2,1)S(1)}, u32[]{:S(2)}, u32[]{:S(2)}) async-start(bf16[16,1,64,256]{3,2,1,0:T(8,128)(2,1)} %fusion.18), calls=%async_computation | async-start | bytes 1048576 | tf_op jit(solution)/shard_map/all_to_all | solution.py:48
  147.3 0.2 reduce-scatter.4.cloned.1.call-start
  147.5 0.0 copy-done.3
  147.6 0.1 reshape.112
  147.6 0.0 copy-done.2
  147.6 0.0 copy-done.4
  147.7 0.1 broadcast_bitcast_fusion
  147.8 13.7 %all-to-all-done = bf16[16,1,64,256]{3,2,1,0:T(8,128)(2,1)S(1)} async-done(((bf16[16,1,64,256]{3,2,1,0:T(8,128)(2,1)}), bf16[16,1,64,256]{3,2,1,0:T(8,128)(2,1)S(1)}, u32[]{:S(2)}, u32[]{:S(2)}) %all-to-all-start) | async-done | bytes 524320 | tf_op jit(solution)/shard_map/all_to_all | solution.py:48
  161.6 0.2 broadcast_multiply_fusion.1
  161.8 0.0 all-gather.2.cloned.1.call-done
  161.8 22.9 %fusion.10 = f32[256,4096]{1,0:T(8,128)} fusion(bf16[4096,4096]{1,0:T(8,128)(2,1)} %mul.83, bf16[1024,256]{1,0:T(8,128)(2,1)S(1)} %bitcast.106, bf16[1,1024,4096]{2,1,0:T(8,128)(2,1)} %all-gather.2.cloned.1.call-done, bf16[4096]{0:T(1024)(128)(2,1)S(1)} %convert_element_type.49), kind=kOutput, calls=%fused_computation.8 | convolution fusion | flops 10739515392 | bytes 46669824 | tf_op jit(solution)/shard_map/scj,ji->sci/dot_general | solution.py:59
  184.7 4.9 %reshape.113 = f32[8192,128]{1,0:T(8,128)} reshape(f32[256,4096]{1,0:T(8,128)} %fusion.10) | data formatting | bytes 8388608 | tf_op jit(solution)/shard_map/reshape | solution.py:61
  189.6 3.2 %gather_fusion = f32[512,128]{1,0:T(8,128)S(1)} fusion(f32[8192,128]{1,0:T(8,128)} %reshape.113, s32[1024]{0:T(1024)S(1)} %pad_clamp_fusion), kind=kCustom, calls=%fused_computation | custom fusion | bytes 526336 | tf_op jit(solution)/shard_map/jit(_take)/gather | solution.py:62
  192.9 0.1 fusion.16
  193.0 0.1 reshape.127
  193.1 15.1 %convolution_bitcast_fusion = f32[256,1]{1,0:T(8,128)} fusion(bf16[65536,1]{0,1:T(2,128)(2,1)S(1)} %reshape.127, bf16[256,65536]{1,0:T(8,128)(2,1)} %param.13), kind=kOutput, calls=%fused_computation.9 | convolution fusion | flops 33554432 | bytes 33686528 | tf_op jit(solution)/shard_map/qc,sc->qs/dot_general | solution.py:65
  208.2 0.0 reduce-scatter.4.cloned.1.call-update
  208.3 1.1 fusion.15
  209.4 54.3 %reduce-scatter.4.cloned.1.call-done = f32[16,1]{1,0:T(8,128)} async-done(((f32[256,1]{1,0:T(8,128)}), f32[16,1]{1,0:T(8,128)}) %reduce-scatter.4.cloned.1.call-update) | async-done | bytes 80
  263.6 1.3 copy.10
  (6 shorter events, 0.1 us)
Async XLA Ops:
  7.2 154.6 %all-gather.2.cloned.1.call-start = ((), (), s32[]{:S(2)}) async-start(), calls=%async_computation.2 | async-start | bytes 8912896 | tf_op jit(solution)/shard_map/all_gather | solution.py:55
  29.1 87.2 %copy-start.1 = (s32[4096]{0:T(1024)S(1)}, s32[4096]{0:T(1024)}, u32[]{:S(2)}) copy-start(s32[4096]{0:T(1024)} %param.11) | copy-start | bytes 49156
  29.1 87.2 %copy-start = (bf16[1,64,4096]{2,1,0:T(8,128)(2,1)S(1)}, bf16[1,64,4096]{2,1,0:T(8,128)(2,1)}, u32[]{:S(2)}) copy-start(bf16[1,64,4096]{2,1,0:T(8,128)(2,1)} %param.7) | copy-start | bytes 1572868
  116.3 31.2 %copy-start.3 = (s32[1,1024]{1,0:T(1,128)S(1)}, s32[1,1024]{1,0:T(1,128)}, u32[]{:S(2)}) copy-start(s32[1,1024]{1,0:T(1,128)} %param.9) | copy-start | bytes 12292
  116.3 31.3 %copy-start.2 = (s32[4096]{0:T(1024)S(1)}, s32[4096]{0:T(1024)}, u32[]{:S(2)}) copy-start(s32[4096]{0:T(1024)} %param.10) | copy-start | bytes 49156
  116.3 31.4 %copy-start.4 = (s32[512]{0:T(512)S(1)}, s32[512]{0:T(512)}, u32[]{:S(2)}) copy-start(s32[512]{0:T(512)} %param.12) | copy-start | bytes 6148
  139.8 21.7 %all-to-all-start = ((bf16[16,1,64,256]{3,2,1,0:T(8,128)(2,1)}), bf16[16,1,64,256]{3,2,1,0:T(8,128)(2,1)S(1)}, u32[]{:S(2)}, u32[]{:S(2)}) async-start(bf16[16,1,64,256]{3,2,1,0:T(8,128)(2,1)} %fusion.18), calls=%async_computation | async-start | bytes 1048576 | tf_op jit(solution)/shard_map/all_to_all | solution.py:48
  147.3 116.3 %reduce-scatter.4.cloned.1.call-start = ((), (), s32[]{:S(2)}) async-start(), calls=%async_computation.3 | async-start | bytes 139264
Sparse Core Ops, SparseCore 0:
  10.1 80.4 all-gather.1
  208.4 55.1 reduce-scatter.3
